TPU v7x, 256 devices: a whole 4x4x8 slice. The times are simulated.
256 devices in a mesh: slab: 4 (over y_hi, core), row: 8 (over x, y_lo), col: 8 (over z).
Axes of the slice: x: 4, y: 4 (y_hi: 2, y_lo: 2; y = y_hi * 2 + y_lo), z: 8, core: 2. Of those that a mesh axis runs over, the one named last changes fastest.
Arguments:
- reflection: bfloat16 [4, 4096, 4096], P('slab', 'row', 'col'), may hold values from -0.0625 to 0.0625
- transmission: bfloat16 [4, 4096, 4096], P('slab', 'row', 'col'), may hold values from -0.09375 to 0.09375
- shots: bfloat16 [4, 4096, 2048], P('slab', 'row', 'col'), may hold values from -6 to 6
Outputs:
- merged: bfloat16 [4, 4096, 2048], P('slab', 'row', 'col')
All inputs are finite; a program needn't handle non-finite values.
Results may differ from a plain program's by a relative error of at most 0.008.
Values may be sent and summed in bfloat16 or wider, within the bound.
No kernel may reach another device: no remote copies, remote signals or barrier semaphores. Data moves between devices by JAX's collectives and lax.ppermute only.
A program may use at most 64 MiB of HBM per device.

v0:
```python
import jax
import jax.numpy as jnp
from jax import lax
from jax.sharding import PartitionSpec as P


def partner(block, axis, bit):
    count = lax.axis_size(axis)
    route = []
    for low in range(count):
        high = low | 1 << bit
        if high != low and high < count:
            route += [(low, high), (high, low)]
    return lax.ppermute(block, axis, route)


def in_order(parts, dim):
    parts = jnp.moveaxis(parts, 0, dim)
    dims = parts.shape
    return parts.reshape(*dims[:dim], dims[dim] * dims[dim + 1], *dims[dim + 2 :])


def from_everyone(array, axis):
    copies = jnp.broadcast_to(array, (lax.axis_size(axis), *array.shape))
    return lax.all_to_all(copies, axis, split_axis=0, concat_axis=0, tiled=True)


def collect(array, axis, dim):
    return in_order(from_everyone(array, axis), dim)


def fold_with(panel, highest, piece):
    if highest:
        return jnp.dot(
            panel.astype(jnp.float32), piece.astype(jnp.float32), precision=lax.Precision.HIGHEST
        )
    return jnp.dot(panel, piece, preferred_element_type=jnp.float32)


def on_device(reflection, transmission, shots):
    own_refl = reflection[0]
    own_trans = transmission[0]
    shot_tile = shots[0]
    far_refl, far_trans = partner((own_refl, own_trans), "slab", 0)
    trans_panel = lax.all_gather(own_trans, "col", axis=1, tiled=True)
    first = fold_with(trans_panel, False, collect(shot_tile, "row", 0)).astype(jnp.bfloat16)
    partner_panel = lax.all_gather(far_refl, "col", axis=1, tiled=True)
    middle = fold_with(partner_panel, False, collect(first, "row", 0))
    own_panel = lax.all_gather(own_refl, "col", axis=1, tiled=True)
    bounce = fold_with(
        own_panel,
        True,
        lax.all_gather(middle.astype(jnp.bfloat16), "row", axis=0, tiled=True).astype(jnp.float32),
    )
    summed = (first.astype(jnp.float32) + bounce).astype(jnp.bfloat16)
    out_panel = lax.all_gather(far_trans, "col", axis=1, tiled=True)
    merged = fold_with(out_panel, False, collect(summed, "row", 0))
    return merged.astype(jnp.bfloat16)[None]


def solution(mesh):
    placed = (P("slab", "row", "col"), P("slab", "row", "col"), P("slab", "row", "col"))
    return jax.shard_map(
        on_device, mesh=mesh, in_specs=placed, out_specs=P("slab", "row", "col"), check_vma=False
    )
```

profile of v0, /device:TPU:1, one launch (start us, length us, event | category | flops | bytes accessed | tf_op | source)
XLA Modules:
  0.0 299.9 jit_solution(3459101234463216938)
XLA Ops:
  6.5 0.0 all-gather.14.cloned.1.call-start
  6.5 0.7 all-gather.14.cloned.1.call-update
  7.3 0.0 all-gather.8.cloned.1.call-start
  7.3 3.3 %collective-permute-start = (bf16[512,512]{1,0:T(8,128)(2,1)}, bf16[512,512]{1,0:T(8,128)(2,1)S(1)}, u32[]{:S(2)}, u32[]{:S(2)}) collective-permute-start(bf16[512,512]{1,0:T(8,128)(2,1)} %bitcast.42), channel_id=1, source_target_pairs={{0,64},{64,0},{128,192},{192,128},{1,65},{65,1},{129,193},{193,129... | collective-permute-start | bytes 1572872 | tf_op jit(solution)/shard_map/ppermute | solution.py:14
  10.6 1.7 collective-permute-done
  12.4 0.0 copy-start.1
  12.4 0.8 copy-done.1
  13.2 0.0 all-gather.8.cloned.1.call-update
  13.3 0.0 all-gather.16.cloned.1.call-start
  13.3 0.7 all-gather.16.cloned.1.call-update
  14.0 1.1 broadcast_in_dim.12
  15.1 28.6 %all_to_all.15 = bf16[8,512,256]{2,1,0:T(8,128)(2,1)S(1)} all-to-all(bf16[8,512,256]{2,1,0:T(8,128)(2,1)S(1)} %broadcast_in_dim.12), channel_id=1, replica_groups=mesh['slab'=4,'row'=8,'col'=8] {'row'}, dimensions={0} | all-to-all | bytes 4194304 | tf_op jit(solution)/shard_map/all_to_all | solution.py:25
  43.7 24.1 %all-gather.14.cloned.1.call-done = bf16[1,512,4096]{2,1,0:T(8,128)(2,1)} async-done(((bf16[1,512,512]{2,1,0:T(8,128)(2,1)}), bf16[1,512,4096]{2,1,0:T(8,128)(2,1)}) %all-gather.14.cloned.1.call-update) | async-done | bytes 4194320 | tf_op jit(solution)/shard_map/all_gather | solution.py:45
  67.8 3.4 %fusion.13 = bf16[512,256]{1,0:T(8,128)(2,1)S(1)} fusion(bf16[4096,256]{1,0:T(8,128)(2,1)S(1)} %bitcast.40, bf16[1,512,4096]{2,1,0:T(8,128)(2,1)} %all-gather.14.cloned.1.call-done), kind=kOutput, calls=%fused_computation.7 | convolution fusion | flops 1073872896 | bytes 6553600 | tf_op jit(solution)/shard_map/dot_general | solution.py:37
  71.2 1.5 broadcast_in_dim.13
  72.8 4.9 %all-to-all-start.1 = ((bf16[8,512,256]{2,1,0:T(8,128)(2,1)}), bf16[8,512,256]{2,1,0:T(8,128)(2,1)S(1)}, u32[]{:S(2)}, u32[]{:S(2)}) async-start(bf16[8,512,256]{2,1,0:T(8,128)(2,1)} %broadcast_in_dim.13), calls=%async_computation.1 | async-start | bytes 4194304 | tf_op jit(solution)/shard_map/all_to_all | solution.py:25
  77.7 0.0 all-gather.10.cloned.1.call-start
  77.7 45.3 %all-gather.8.cloned.1.call-done = bf16[512,4096]{1,0:T(8,128)(2,1)} async-done(((bf16[512,512]{1,0:T(8,128)(2,1)}), bf16[512,4096]{1,0:T(8,128)(2,1)}) %all-gather.8.cloned.1.call-update) | async-done | bytes 4194320 | tf_op jit(solution)/shard_map/all_gather | solution.py:47
  123.1 0.0 all-to-all-done.1
  123.1 0.0 copy-start
  123.1 4.2 %fusion.16 = bf16[512,256]{0,1:T(8,128)(2,1)} fusion(bf16[4096,256]{1,0:T(8,128)(2,1)S(1)} %bitcast.38, bf16[512,4096]{1,0:T(8,128)(2,1)} %all-gather.8.cloned.1.call-done), kind=kOutput, calls=%fused_computation.10 | convolution fusion | flops 1073872896 | bytes 6553600 | tf_op jit(solution)/shard_map/dot_general | solution.py:37
  127.3 0.0 all-gather.10.cloned.1.call-update
  127.3 0.0 all-gather.12.cloned.1.call-start
  127.4 0.0 copy-done
  127.4 0.8 collective-permute-start.1
  128.2 1.5 collective-permute-done.1
  129.7 0.0 copy-start.2
  129.7 0.8 copy-done.2
  130.5 0.0 all-gather.12.cloned.1.call-update
  130.5 47.8 %all-gather.16.cloned.1.call-done = bf16[1,512,4096]{2,1,0:T(8,128)(2,1)} async-done(((bf16[1,512,512]{2,1,0:T(8,128)(2,1)}), bf16[1,512,4096]{2,1,0:T(8,128)(2,1)}) %all-gather.16.cloned.1.call-update) | async-done | bytes 4194320 | tf_op jit(solution)/shard_map/all_gather | solution.py:49
  178.3 53.4 %all-gather.10.cloned.1.call-done = bf16[4096,256]{0,1:T(8,128)(2,1)} async-done(((bf16[512,256]{0,1:T(8,128)(2,1)}), bf16[4096,256]{0,1:T(8,128)(2,1)}) %all-gather.10.cloned.1.call-update) | async-done | bytes 2097168 | tf_op jit(solution)/shard_map/all_gather | solution.py:53
  231.7 4.1 %fusion.10 = bf16[512,256]{1,0:T(8,128)(2,1)S(1)} fusion(bf16[4096,256]{0,1:T(8,128)(2,1)} %all-gather.10.cloned.1.call-done, bf16[1,512,4096]{2,1,0:T(8,128)(2,1)} %all-gather.16.cloned.1.call-done, bf16[512,256]{1,0:T(8,128)(2,1)S(1)} %fusion.13), kind=kOutput, calls=%fused_computation.6 | convolution fusion | flops 1074135040 | bytes 6815744 | tf_op jit(solution)/shard_map/dot_general | solution.py:34
  235.8 1.5 broadcast_in_dim.14
  237.3 4.5 %all-to-all-start.2 = ((bf16[8,512,256]{2,1,0:T(8,128)(2,1)}), bf16[8,512,256]{2,1,0:T(8,128)(2,1)S(1)}, u32[]{:S(2)}, u32[]{:S(2)}) async-start(bf16[8,512,256]{2,1,0:T(8,128)(2,1)} %broadcast_in_dim.14), calls=%async_computation.2 | async-start | bytes 4194304 | tf_op jit(solution)/shard_map/all_to_all | solution.py:25
  241.8 47.3 %all-gather.12.cloned.1.call-done = bf16[512,4096]{1,0:T(8,128)(2,1)} async-done(((bf16[512,512]{1,0:T(8,128)(2,1)}), bf16[512,4096]{1,0:T(8,128)(2,1)}) %all-gather.12.cloned.1.call-update) | async-done | bytes 4194320 | tf_op jit(solution)/shard_map/all_gather | solution.py:56
  289.0 0.0 all-to-all-done.2
  289.0 3.5 %fusion.17 = bf16[1,512,256]{1,2,0:T(8,128)(2,1)S(1)} fusion(bf16[4096,256]{1,0:T(8,128)(2,1)S(1)} %bitcast.39, bf16[512,4096]{1,0:T(8,128)(2,1)} %all-gather.12.cloned.1.call-done), kind=kOutput, calls=%fused_computation.11 | convolution fusion | flops 1073872896 | bytes 6553600 | tf_op jit(solution)/shard_map/dot_general | solution.py:37
  292.5 0.8 copy.5
Async XLA Ops:
  6.5 61.3 %all-gather.14.cloned.1.call-start = ((), (), s32[]{:S(2)}) async-start(), calls=%async_computation.6 | async-start | bytes 4718592 | tf_op jit(solution)/shard_map/all_gather | solution.py:45
  7.3 115.8 %all-gather.8.cloned.1.call-start = ((), (), s32[]{:S(2)}) async-start(), calls=%async_computation.3 | async-start | bytes 4718592 | tf_op jit(solution)/shard_map/all_gather | solution.py:47
  7.3 5.1 %collective-permute-start = (bf16[512,512]{1,0:T(8,128)(2,1)}, bf16[512,512]{1,0:T(8,128)(2,1)S(1)}, u32[]{:S(2)}, u32[]{:S(2)}) collective-permute-start(bf16[512,512]{1,0:T(8,128)(2,1)} %bitcast.42), channel_id=1, source_target_pairs={{0,64},{64,0},{128,192},{192,128},{1,65},{65,1},{129,193},{193,129... | collective-permute-start | bytes 1572872 | tf_op jit(solution)/shard_map/ppermute | solution.py:14
  12.4 0.9 copy-start.1
  13.3 165.1 %all-gather.16.cloned.1.call-start = ((), (), s32[]{:S(2)}) async-start(), calls=%async_computation.7 | async-start | bytes 4718592 | tf_op jit(solution)/shard_map/all_gather | solution.py:49
  72.8 50.3 %all-to-all-start.1 = ((bf16[8,512,256]{2,1,0:T(8,128)(2,1)}), bf16[8,512,256]{2,1,0:T(8,128)(2,1)S(1)}, u32[]{:S(2)}, u32[]{:S(2)}) async-start(bf16[8,512,256]{2,1,0:T(8,128)(2,1)} %broadcast_in_dim.13), calls=%async_computation.1 | async-start | bytes 4194304 | tf_op jit(solution)/shard_map/all_to_all | solution.py:25
  77.7 154.0 %all-gather.10.cloned.1.call-start = ((), (), s32[]{:S(2)}) async-start(), calls=%async_computation.4 | async-start | bytes 2359296 | tf_op jit(solution)/shard_map/all_gather | solution.py:53
  123.1 4.3 %copy-start = (bf16[1,512,512]{2,1,0:T(8,128)(2,1)S(1)}, bf16[1,512,512]{2,1,0:T(8,128)(2,1)}, u32[]{:S(2)}) copy-start(bf16[1,512,512]{2,1,0:T(8,128)(2,1)} %param.4) | copy-start | bytes 1572868
  127.3 161.7 %all-gather.12.cloned.1.call-start = ((), (), s32[]{:S(2)}) async-start(), calls=%async_computation.5 | async-start | bytes 4718592 | tf_op jit(solution)/shard_map/all_gather | solution.py:56
  127.4 2.3 collective-permute-start.1
  129.7 0.8 copy-start.2
  237.3 51.8 %all-to-all-start.2 = ((bf16[8,512,256]{2,1,0:T(8,128)(2,1)}), bf16[8,512,256]{2,1,0:T(8,128)(2,1)S(1)}, u32[]{:S(2)}, u32[]{:S(2)}) async-start(bf16[8,512,256]{2,1,0:T(8,128)(2,1)} %broadcast_in_dim.14), calls=%async_computation.2 | async-start | bytes 4194304 | tf_op jit(solution)/shard_map/all_to_all | solution.py:25
Sparse Core Ops, SparseCore 0:
  9.1 58.6 all-gather.13
  69.6 53.4 all-gather.7
  124.9 53.4 all-gather.15
  180.0 51.6 all-gather.9
  233.3 55.6 all-gather.11
where the time goes:
time: 300 us
  waiting for transfers between devices  223 us (74%)
  blocking collectives  28.6 us (10%)
  matrix products  15.3 us (5%)
  starting transfers between devices  13.7 us (5%)
  between operations  13.2 us (4%)
  local copies, waits for them, and re-layouts  6.57 us (2%)
    all_gather x1, waiting for transfers between devices, on_device(): lax.all_gather(middle.astype(jnp.bfloat16), 'row', axis=0, tiled=True)  53.4 us
    all_gather x1, waiting for transfers between devices, on_device(): own_panel = lax.all_gather(own_refl, 'col', axis=1, tiled=True)  47.8 us
    all_gather x1, waiting for transfers between devices, on_device(): out_panel = lax.all_gather(far_trans, 'col', axis=1, tiled=True)  47.3 us
    all_gather x1, waiting for transfers between devices, on_device(): partner_panel = lax.all_gather(far_refl, 'col', axis=1, tiled=True)  45.3 us
    all_to_all x1, blocking collectives, from_everyone(): return lax.all_to_all(copies, axis, split_axis=0, concat_axis=0, tiled=True)  28.6 us
    all_gather x1, waiting for transfers between devices, on_device(): trans_panel = lax.all_gather(own_trans, 'col', axis=1, tiled=True)  24.1 us
    dot_general x3, matrix products, fold_with(): return jnp.dot(panel, piece, preferred_element_type=jnp.float32)  11.2 us
    all_to_all x2, starting transfers between devices, from_everyone(): return lax.all_to_all(copies, axis, split_axis=0, concat_axis=0, tiled=True)  9.41 us
  transfers between devices with their start and end apart: 9, of which 7 were waited for; matrix products, arithmetic and copies ran while one was open for 5% of the time, Pallas kernels for 0%

commit v1 on v0

--- a/solution.py
+++ b/solution.py
@@ -2,6 +2,35 @@
 import jax.numpy as jnp
 from jax import lax
 from jax.sharding import PartitionSpec as P
+
+
+def note_rates_for(block_here, group_axis):
+    left_arr = lax.axis_size(group_axis)
+    w2 = lax.axis_index(group_axis)
+    bank = []
+    new, arr_out, raw_out = (left_arr, w2, block_here.shape[1])
+    for pp, s in enumerate(block_here.shape):
+        bank.append(s * new if pp == 1 else s)
+    m_next = jnp.zeros(bank, block_here.dtype)
+    latest = carry_out = block_here
+    base_arr = lax.dynamic_update_slice_in_dim(m_next, block_here, arr_out * raw_out, axis=1)
+    for at in range(1, new // 2 + 1):
+        pages = []
+        for pp in range(new):
+            pages.append((pp, (pp + 1) % new))
+        latest = lax.ppermute(latest, axis_name=group_axis, perm=pages)
+        base_arr = lax.dynamic_update_slice_in_dim(
+            base_arr, latest, (arr_out - at) % new * raw_out, axis=1
+        )
+        if 2 * at < new:
+            grid = []
+            for pp in range(new):
+                grid.append((pp, (pp - 1) % new))
+            carry_out = lax.ppermute(carry_out, axis_name=group_axis, perm=grid)
+            base_arr = lax.dynamic_update_slice_in_dim(
+                base_arr, carry_out, (arr_out + at) % new * raw_out, axis=1
+            )
+    return base_arr
 
 
 def partner(block, axis, bit):
@@ -46,7 +75,7 @@
     first = fold_with(trans_panel, False, collect(shot_tile, "row", 0)).astype(jnp.bfloat16)
     partner_panel = lax.all_gather(far_refl, "col", axis=1, tiled=True)
     middle = fold_with(partner_panel, False, collect(first, "row", 0))
-    own_panel = lax.all_gather(own_refl, "col", axis=1, tiled=True)
+    own_panel = note_rates_for(own_refl, "col")
     bounce = fold_with(
         own_panel,
         True,

time: 300 us -> 248 us (0.83)
  waiting for transfers between devices: 223 us -> 151 us
  local copies, waits for them, and re-layouts: 6.57 us -> 16.3 us
  starting transfers between devices: 13.7 us -> 22.6 us
    all_gather x1, waiting for transfers between devices: 53.4 us -> 0.01 us  [on_device(): lax.all_gather(middle.astype(jnp.bfloat16), 'row', axis=0, tiled=True)]
    all_gather x1 -> x0, waiting for transfers between devices: 47.8 us -> none  [on_device(): own_panel = lax.all_gather(own_refl, 'col', axis=1, tiled=True)]
    ppermute x0 -> x7, waiting for transfers between devices: none -> 35.2 us  [the longest x4 35.2 us: note_rates_for(): latest = lax.ppermute(latest, axis_name=group_axis, perm=pages)]
    ppermute x0 -> x7, starting transfers between devices: none -> 8.12 us  [the longest x3 8.03 us: note_rates_for(): carry_out = lax.ppermute(carry_out, axis_name=group_axis, perm=grid)]
    dynamic_update_slice x0 -> x8, local copies, waits for them, and re-layouts: none -> 7.17 us  [the longest x4 3.7 us: note_rates_for(): lax.dynamic_update_slice_in_dim(base_arr, latest, (arr_out - at) % new *...]
    all_gather x1, waiting for transfers between devices: 47.3 us -> 42 us  [on_device(): out_panel = lax.all_gather(far_trans, 'col', axis=1, tiled=True)]
  transfers between devices with their start and end apart: 9 -> 15, of which waited for: 7 -> 9; matrix products, arithmetic and copies ran while one was open for 5% -> 9% of each run, Pallas kernels for 0% -> 0%
where the time goes in v1:
time: 248 us; the launch traced here: 247 us
  waiting for transfers between devices  151 us (61%)
  blocking collectives  28.6 us (12%)
  starting transfers between devices  22.6 us (9%)
  local copies, waits for them, and re-layouts  16.3 us (7%)
  matrix products  15.3 us (6%)
  between operations  13.2 us (5%)
    all_gather x1, waiting for transfers between devices, on_device(): partner_panel = lax.all_gather(far_refl, 'col', axis=1, tiled=True)  45.4 us
    all_gather x1, waiting for transfers between devices, on_device(): out_panel = lax.all_gather(far_trans, 'col', axis=1, tiled=True)  42 us
    ppermute x4, waiting for transfers between devices, note_rates_for(): latest = lax.ppermute(latest, axis_name=group_axis, perm=pages)  35.2 us
    all_to_all x1, blocking collectives, from_everyone(): return lax.all_to_all(copies, axis, split_axis=0, concat_axis=0, tiled=True)  28.6 us
    all_gather x1, waiting for transfers between devices, on_device(): trans_panel = lax.all_gather(own_trans, 'col', axis=1, tiled=True)  24.8 us
    dot_general x3, matrix products, fold_with(): return jnp.dot(panel, piece, preferred_element_type=jnp.float32)  11.2 us
    all_to_all x2, starting transfers between devices, from_everyone(): return lax.all_to_all(copies, axis, split_axis=0, concat_axis=0, tiled=True)  10.2 us
    ppermute x3, starting transfers between devices, note_rates_for(): carry_out = lax.ppermute(carry_out, axis_name=group_axis, perm=grid)  8.03 us
  transfers between devices with their start and end apart: 15, of which 9 were waited for; matrix products, arithmetic and copies ran while one was open for 9% of the time, Pallas kernels for 0%

profile of v1, /device:TPU:1, one launch (start us, length us, event | category | flops | bytes accessed | tf_op | source)
XLA Modules:
  0.0 247.4 jit_solution(2766846508178069135)
XLA Ops:
  6.5 0.7 all-gather.12.cloned.1.call-update
  7.3 0.0 all-gather.6.cloned.1.call-start
  7.3 3.3 %collective-permute-start.7 = (bf16[512,512]{1,0:T(8,128)(2,1)}, bf16[512,512]{1,0:T(8,128)(2,1)S(1)}, u32[]{:S(2)}, u32[]{:S(2)}) collective-permute-start(bf16[512,512]{1,0:T(8,128)(2,1)} %bitcast.29), channel_id=1, source_target_pairs={{0,64},{64,0},{128,192},{192,128},{1,65},{65,1},{129,193},{193,129... | collective-permute-start | bytes 1572872 | tf_op jit(solution)/shard_map/ppermute | solution.py:43
  10.6 1.7 collective-permute-done.7
  12.4 0.9 copy-done.2
  13.2 0.0 all-gather.6.cloned.1.call-update
  13.3 1.1 broadcast_in_dim.15
  14.4 28.6 %all_to_all.15 = bf16[8,512,256]{2,1,0:T(8,128)(2,1)S(1)} all-to-all(bf16[8,512,256]{2,1,0:T(8,128)(2,1)S(1)} %broadcast_in_dim.15), channel_id=1, replica_groups=mesh['slab'=4,'row'=8,'col'=8] {'row'}, dimensions={0} | all-to-all | bytes 4194304 | tf_op jit(solution)/shard_map/all_to_all | solution.py:54
  43.0 24.8 %all-gather.12.cloned.1.call-done = bf16[1,512,4096]{2,1,0:T(8,128)(2,1)} async-done(((bf16[1,512,512]{2,1,0:T(8,128)(2,1)}), bf16[1,512,4096]{2,1,0:T(8,128)(2,1)}) %all-gather.12.cloned.1.call-update) | async-done | bytes 4194320 | tf_op jit(solution)/shard_map/all_gather | solution.py:74
  67.8 3.4 %fusion.3 = bf16[512,256]{1,0:T(8,128)(2,1)S(1)} fusion(bf16[4096,256]{1,0:T(8,128)(2,1)S(1)} %bitcast.27, bf16[1,512,4096]{2,1,0:T(8,128)(2,1)} %all-gather.12.cloned.1.call-done), kind=kOutput, calls=%fused_computation.4 | convolution fusion | flops 1073872896 | bytes 6553600 | tf_op jit(solution)/shard_map/dot_general | solution.py:66
  71.2 1.5 broadcast_in_dim.17
  72.7 4.9 %all-to-all-start.1 = ((bf16[8,512,256]{2,1,0:T(8,128)(2,1)}), bf16[8,512,256]{2,1,0:T(8,128)(2,1)S(1)}, u32[]{:S(2)}, u32[]{:S(2)}) async-start(bf16[8,512,256]{2,1,0:T(8,128)(2,1)} %broadcast_in_dim.17), calls=%async_computation.1 | async-start | bytes 4194304 | tf_op jit(solution)/shard_map/all_to_all | solution.py:54
  77.6 0.0 all-gather.8.cloned.1.call-start
  77.7 45.4 %all-gather.6.cloned.1.call-done = bf16[512,4096]{1,0:T(8,128)(2,1)} async-done(((bf16[512,512]{1,0:T(8,128)(2,1)}), bf16[512,4096]{1,0:T(8,128)(2,1)}) %all-gather.6.cloned.1.call-update) | async-done | bytes 4194320 | tf_op jit(solution)/shard_map/all_gather | solution.py:76
  123.1 4.2 %fusion.6 = bf16[512,256]{0,1:T(8,128)(2,1)} fusion(bf16[4096,256]{1,0:T(8,128)(2,1)S(1)} %bitcast.25, bf16[512,4096]{1,0:T(8,128)(2,1)} %all-gather.6.cloned.1.call-done), kind=kOutput, calls=%fused_computation.7 | convolution fusion | flops 1073872896 | bytes 6553600 | tf_op jit(solution)/shard_map/dot_general | solution.py:66
  127.3 0.0 all-gather.8.cloned.1.call-update
  127.3 0.0 all-gather.10.cloned.1.call-start
  127.4 0.8 collective-permute-start.8
  128.2 1.5 collective-permute-done.8
  129.7 0.8 copy-done.1
  130.5 0.0 all-gather.10.cloned.1.call-update
  130.5 0.1 collective-permute-start
  130.6 2.7 %collective-permute-start.1 = (bf16[512,512]{1,0:T(8,128)(2,1)S(1)}, bf16[512,512]{1,0:T(8,128)(2,1)S(1)}, u32[]{:S(2)}, u32[]{:S(2)}) collective-permute-start(bf16[512,512]{1,0:T(8,128)(2,1)S(1)} %bitcast.31), channel_id=1, source_target_pairs={{0,7},{1,0},{2,1},{3,2},{4,3},{5,4},{6,5},{7,6},{8,15},{9,8},{10,9... | collective-permute-start | bytes 1572872 | tf_op jit(solution)/shard_map/ppermute | solution.py:29
  133.3 11.7 %collective-permute-done = bf16[512,512]{1,0:T(8,128)(2,1)S(1)} collective-permute-done((bf16[512,512]{1,0:T(8,128)(2,1)S(1)}, bf16[512,512]{1,0:T(8,128)(2,1)S(1)}, u32[]{:S(2)}, u32[]{:S(2)}) %collective-permute-start) | collective-permute-done | bytes 524320 | tf_op jit(solution)/shard_map/ppermute | solution.py:21
  145.0 2.7 %collective-permute-start.3 = (bf16[512,512]{1,0:T(8,128)(2,1)S(1)}, bf16[512,512]{1,0:T(8,128)(2,1)S(1)}, u32[]{:S(2)}, u32[]{:S(2)}) collective-permute-start(bf16[512,512]{1,0:T(8,128)(2,1)S(1)} %collective-permute-done.1), channel_id=1, source_target_pairs={{0,7},{1,0},{2,1},{3,2},{4,3},{5,4},{6,5},{7,6},{8,15},{9,8},{10,9... | collective-permute-start | bytes 1572872 | tf_op jit(solution)/shard_map/ppermute | solution.py:29
  147.6 10.7 %collective-permute-done.2 = bf16[512,512]{1,0:T(8,128)(2,1)S(1)} collective-permute-done((bf16[512,512]{1,0:T(8,128)(2,1)S(1)}, bf16[512,512]{1,0:T(8,128)(2,1)S(1)}, u32[]{:S(2)}, u32[]{:S(2)}) %collective-permute-start.2) | collective-permute-done | bytes 524320 | tf_op jit(solution)/shard_map/ppermute | solution.py:21
  158.4 2.5 %broadcast_in_dim.16 = bf16[512,4096]{1,0:T(8,128)(2,1)} broadcast(bf16[]{:T(256)} %constant.49.clone.1), dimensions={} | broadcast | bytes 4194306 | tf_op jit(solution)/shard_map/broadcast_in_dim | solution.py:14
  160.9 0.9 constant_dynamic-update-slice_fusion.7
  161.8 0.0 collective-permute-done.3
  161.8 2.7 %collective-permute-start.5 = (bf16[512,512]{1,0:T(8,128)(2,1)S(1)}, bf16[512,512]{1,0:T(8,128)(2,1)S(1)}, u32[]{:S(2)}, u32[]{:S(2)}) collective-permute-start(bf16[512,512]{1,0:T(8,128)(2,1)S(1)} %collective-permute-done.3), channel_id=1, source_target_pairs={{0,7},{1,0},{2,1},{3,2},{4,3},{5,4},{6,5},{7,6},{8,15},{9,8},{10,9... | collective-permute-start | bytes 1572872 | tf_op jit(solution)/shard_map/ppermute | solution.py:29
  164.5 0.9 constant_dynamic-update-slice_fusion.6
  165.4 5.6 %collective-permute-done.4 = bf16[512,512]{1,0:T(8,128)(2,1)S(1)} collective-permute-done((bf16[512,512]{1,0:T(8,128)(2,1)S(1)}, bf16[512,512]{1,0:T(8,128)(2,1)S(1)}, u32[]{:S(2)}, u32[]{:S(2)}) %collective-permute-start.4) | collective-permute-done | bytes 524320 | tf_op jit(solution)/shard_map/ppermute | solution.py:21
  171.0 0.0 collective-permute-start.6
  171.0 0.9 constant_dynamic-update-slice_fusion.5
  171.9 0.9 constant_dynamic-update-slice_fusion.4
  172.8 0.9 constant_dynamic-update-slice_fusion.3
  173.7 1.0 constant_dynamic-update-slice_fusion.2
  174.6 0.0 collective-permute-done.5
  174.6 0.8 constant_dynamic-update-slice_fusion.1
  175.5 7.2 %collective-permute-done.6 = bf16[512,512]{1,0:T(8,128)(2,1)S(1)} collective-permute-done((bf16[512,512]{1,0:T(8,128)(2,1)S(1)}, bf16[512,512]{1,0:T(8,128)(2,1)S(1)}, u32[]{:S(2)}, u32[]{:S(2)}) %collective-permute-start.6) | collective-permute-done | bytes 524320 | tf_op jit(solution)/shard_map/ppermute | solution.py:21
  182.7 0.9 constant_dynamic-update-slice_fusion
  183.6 4.1 %fusion.2 = bf16[512,256]{1,0:T(8,128)(2,1)S(1)} fusion(bf16[512,4096]{1,0:T(8,128)(2,1)} %constant_dynamic-update-slice_fusion, bf16[4096,256]{0,1:T(8,128)(2,1)} %all-gather.8.cloned.1.call-done, bf16[512,256]{1,0:T(8,128)(2,1)S(1)} %fusion.3), kind=kOutput, calls=%fused_computation.3 | convolution fusion | flops 1074135040 | bytes 6815744 | tf_op jit(solution)/shard_map/dot_general | solution.py:63
  187.8 1.5 broadcast_in_dim.18
  189.2 5.3 %all-to-all-start.2 = ((bf16[8,512,256]{2,1,0:T(8,128)(2,1)}), bf16[8,512,256]{2,1,0:T(8,128)(2,1)S(1)}, u32[]{:S(2)}, u32[]{:S(2)}) async-start(bf16[8,512,256]{2,1,0:T(8,128)(2,1)} %broadcast_in_dim.18), calls=%async_computation.2 | async-start | bytes 4194304 | tf_op jit(solution)/shard_map/all_to_all | solution.py:54
  194.6 42.0 %all-gather.10.cloned.1.call-done = bf16[512,4096]{1,0:T(8,128)(2,1)} async-done(((bf16[512,512]{1,0:T(8,128)(2,1)}), bf16[512,4096]{1,0:T(8,128)(2,1)}) %all-gather.10.cloned.1.call-update) | async-done | bytes 4194320 | tf_op jit(solution)/shard_map/all_gather | solution.py:85
  236.5 0.0 all-to-all-done.2
  236.5 3.5 %fusion.7 = bf16[1,512,256]{1,2,0:T(8,128)(2,1)S(1)} fusion(bf16[4096,256]{1,0:T(8,128)(2,1)S(1)} %bitcast.26, bf16[512,4096]{1,0:T(8,128)(2,1)} %all-gather.10.cloned.1.call-done), kind=kOutput, calls=%fused_computation.8 | convolution fusion | flops 1073872896 | bytes 6553600 | tf_op jit(solution)/shard_map/dot_general | solution.py:66
  240.0 0.8 copy.4
  (12 shorter events, 0.0 us)
Async XLA Ops:
  6.5 61.3 %all-gather.12.cloned.1.call-start = ((), (), s32[]{:S(2)}) async-start(), calls=%async_computation.6 | async-start | bytes 4718592 | tf_op jit(solution)/shard_map/all_gather | solution.py:74
  7.3 115.8 %all-gather.6.cloned.1.call-start = ((), (), s32[]{:S(2)}) async-start(), calls=%async_computation.3 | async-start | bytes 4718592 | tf_op jit(solution)/shard_map/all_gather | solution.py:76
  7.3 5.1 %collective-permute-start.7 = (bf16[512,512]{1,0:T(8,128)(2,1)}, bf16[512,512]{1,0:T(8,128)(2,1)S(1)}, u32[]{:S(2)}, u32[]{:S(2)}) collective-permute-start(bf16[512,512]{1,0:T(8,128)(2,1)} %bitcast.29), channel_id=1, source_target_pairs={{0,64},{64,0},{128,192},{192,128},{1,65},{65,1},{129,193},{193,129... | collective-permute-start | bytes 1572872 | tf_op jit(solution)/shard_map/ppermute | solution.py:43
  12.4 0.9 copy-start.2
  72.7 50.3 %all-to-all-start.1 = ((bf16[8,512,256]{2,1,0:T(8,128)(2,1)}), bf16[8,512,256]{2,1,0:T(8,128)(2,1)S(1)}, u32[]{:S(2)}, u32[]{:S(2)}) async-start(bf16[8,512,256]{2,1,0:T(8,128)(2,1)} %broadcast_in_dim.17), calls=%async_computation.1 | async-start | bytes 4194304 | tf_op jit(solution)/shard_map/all_to_all | solution.py:54
  77.6 49.8 %copy-start = (bf16[1,512,512]{2,1,0:T(8,128)(2,1)S(1)}, bf16[1,512,512]{2,1,0:T(8,128)(2,1)}, u32[]{:S(2)}) copy-start(bf16[1,512,512]{2,1,0:T(8,128)(2,1)} %param.4) | copy-start | bytes 1572868
  77.6 106.0 %all-gather.8.cloned.1.call-start = ((), (), s32[]{:S(2)}) async-start(), calls=%async_computation.4 | async-start | bytes 2359296 | tf_op jit(solution)/shard_map/all_gather | solution.py:82
  123.1 7.5 %copy-start.3 = (bf16[1,512,512]{2,1,0:T(8,128)(2,1)S(1)}, bf16[1,512,512]{2,1,0:T(8,128)(2,1)}, u32[]{:S(2)}) copy-start(bf16[1,512,512]{2,1,0:T(8,128)(2,1)} %param.3) | copy-start | bytes 1572868
  127.3 109.2 %all-gather.10.cloned.1.call-start = ((), (), s32[]{:S(2)}) async-start(), calls=%async_computation.5 | async-start | bytes 4718592 | tf_op jit(solution)/shard_map/all_gather | solution.py:85
  127.4 2.3 collective-permute-start.8
  129.7 0.8 copy-start.1
  130.5 14.4 %collective-permute-start = (bf16[512,512]{1,0:T(8,128)(2,1)S(1)}, bf16[512,512]{1,0:T(8,128)(2,1)S(1)}, u32[]{:S(2)}, u32[]{:S(2)}) collective-permute-start(bf16[512,512]{1,0:T(8,128)(2,1)S(1)} %bitcast.30), channel_id=1, source_target_pairs={{0,1},{1,2},{2,3},{3,4},{4,5},{5,6},{6,7},{7,0},{8,9},{9,10},{10,1... | collective-permute-start | bytes 1572872 | tf_op jit(solution)/shard_map/ppermute | solution.py:21
  130.6 14.3 %collective-permute-start.1 = (bf16[512,512]{1,0:T(8,128)(2,1)S(1)}, bf16[512,512]{1,0:T(8,128)(2,1)S(1)}, u32[]{:S(2)}, u32[]{:S(2)}) collective-permute-start(bf16[512,512]{1,0:T(8,128)(2,1)S(1)} %bitcast.31), channel_id=1, source_target_pairs={{0,7},{1,0},{2,1},{3,2},{4,3},{5,4},{6,5},{7,6},{8,15},{9,8},{10,9... | collective-permute-start | bytes 1572872 | tf_op jit(solution)/shard_map/ppermute | solution.py:29
  145.0 13.4 %collective-permute-start.2 = (bf16[512,512]{1,0:T(8,128)(2,1)S(1)}, bf16[512,512]{1,0:T(8,128)(2,1)S(1)}, u32[]{:S(2)}, u32[]{:S(2)}) collective-permute-start(bf16[512,512]{1,0:T(8,128)(2,1)S(1)} %collective-permute-done), channel_id=1, source_target_pairs={{0,1},{1,2},{2,3},{3,4},{4,5},{5,6},{6,7},{7,0},{8,9},{9,10},{10,1... | collective-permute-start | bytes 1572872 | tf_op jit(solution)/shard_map/ppermute | solution.py:21
  145.0 16.9 %collective-permute-start.3 = (bf16[512,512]{1,0:T(8,128)(2,1)S(1)}, bf16[512,512]{1,0:T(8,128)(2,1)S(1)}, u32[]{:S(2)}, u32[]{:S(2)}) collective-permute-start(bf16[512,512]{1,0:T(8,128)(2,1)S(1)} %collective-permute-done.1), channel_id=1, source_target_pairs={{0,7},{1,0},{2,1},{3,2},{4,3},{5,4},{6,5},{7,6},{8,15},{9,8},{10,9... | collective-permute-start | bytes 1572872 | tf_op jit(solution)/shard_map/ppermute | solution.py:29
  158.4 12.6 %collective-permute-start.4 = (bf16[512,512]{1,0:T(8,128)(2,1)S(1)}, bf16[512,512]{1,0:T(8,128)(2,1)S(1)}, u32[]{:S(2)}, u32[]{:S(2)}) collective-permute-start(bf16[512,512]{1,0:T(8,128)(2,1)S(1)} %collective-permute-done.2), channel_id=1, source_target_pairs={{0,1},{1,2},{2,3},{3,4},{4,5},{5,6},{6,7},{7,0},{8,9},{9,10},{10,1... | collective-permute-start | bytes 1572872 | tf_op jit(solution)/shard_map/ppermute | solution.py:21
  161.8 12.8 %collective-permute-start.5 = (bf16[512,512]{1,0:T(8,128)(2,1)S(1)}, bf16[512,512]{1,0:T(8,128)(2,1)S(1)}, u32[]{:S(2)}, u32[]{:S(2)}) collective-permute-start(bf16[512,512]{1,0:T(8,128)(2,1)S(1)} %collective-permute-done.3), channel_id=1, source_target_pairs={{0,7},{1,0},{2,1},{3,2},{4,3},{5,4},{6,5},{7,6},{8,15},{9,8},{10,9... | collective-permute-start | bytes 1572872 | tf_op jit(solution)/shard_map/ppermute | solution.py:29
  171.0 11.7 %collective-permute-start.6 = (bf16[512,512]{1,0:T(8,128)(2,1)S(1)}, bf16[512,512]{1,0:T(8,128)(2,1)S(1)}, u32[]{:S(2)}, u32[]{:S(2)}) collective-permute-start(bf16[512,512]{1,0:T(8,128)(2,1)S(1)} %collective-permute-done.4), channel_id=1, source_target_pairs={{0,1},{1,2},{2,3},{3,4},{4,5},{5,6},{6,7},{7,0},{8,9},{9,10},{10,1... | collective-permute-start | bytes 1572872 | tf_op jit(solution)/shard_map/ppermute | solution.py:21
  189.2 47.3 %all-to-all-start.2 = ((bf16[8,512,256]{2,1,0:T(8,128)(2,1)}), bf16[8,512,256]{2,1,0:T(8,128)(2,1)S(1)}, u32[]{:S(2)}, u32[]{:S(2)}) async-start(bf16[8,512,256]{2,1,0:T(8,128)(2,1)} %broadcast_in_dim.18), calls=%async_computation.2 | async-start | bytes 4194304 | tf_op jit(solution)/shard_map/all_to_all | solution.py:54
Sparse Core Ops, SparseCore 0:
  9.1 58.6 all-gather.11
  69.6 53.4 all-gather.5
  127.5 51.0 all-gather.7
  180.2 56.3 all-gather.9
